TPU v7x, 32 devices: a whole 2x2x4 slice. The times are simulated.
32 devices in a mesh: seq: 8 (over z, x), fsdp: 4 (over y, core).
Axes of the slice: x: 2, y: 2, z: 4, core: 2. Of those that a mesh axis runs over, the one named last changes fastest.
Arguments:
- inputs: bfloat16 [4, 1024, 768], P('fsdp', 'seq'), may hold values from -6 to 6
- cotangent: bfloat16 [4, 1024, 768], P('fsdp', 'seq'), may hold values from -6 to 6
- inproj: bfloat16 [1, 768, 3352], P(None, 'fsdp'), may hold values from -0.21875 to 0.21875
- outproj: bfloat16 [1, 1536, 768], P(None, 'fsdp'), may hold values from -0.15625 to 0.15625
- norm_gain: float32 [1, 768], replicated, may hold values from 0.5 to 2
- gate_gain: float32 [1, 1536], replicated, may hold values from 0.5 to 2
- conv_weight: float32 [1, 4, 1792], replicated, may hold values from -3 to 3
- conv_bias: float32 [1, 1792], replicated, may hold values from -0.5 to 0.5
- step_bias: float32 [1, 24], replicated, may hold values from -5.5 to -4.5
- log_rate: float32 [1, 24], replicated, may hold values from -7 to 1.5
- skip_gain: float32 [1, 24], replicated, may hold values from 0.5 to 2
Outputs:
- output: bfloat16 [4, 1024, 768], P('fsdp', 'seq')
- input_grad: bfloat16 [4, 1024, 768], P('fsdp', 'seq')
- inproj_grad: float32 [1, 768, 3352], P(None, 'fsdp')
- outproj_grad: float32 [1, 1536, 768], P(None, 'fsdp')
- norm_grad: float32 [1, 768], replicated
- gate_grad: float32 [1, 1536], replicated
- kernel_grad: float32 [1, 4, 1792], replicated
- bias_grad: float32 [1, 1792], replicated
- step_grad: float32 [1, 24], replicated
- rate_grad: float32 [1, 24], replicated
- skip_grad: float32 [1, 24], replicated
All inputs are finite; a program needn't handle non-finite values.
Results may differ from a plain program's by a relative error of at most 0.01.
Values may be sent and summed in bfloat16 or wider, within the bound.
A program may use at most 192 MiB of HBM per device.

v0:
```python
import jax
import jax.numpy as jnp
from jax import lax
from jax.sharding import PartitionSpec as P

H = 24
P_SIZE = 64
N = 128
CONV = 4
SPAN = 64
LAYERS = 1
DI = 1536
XBC = 1792
epsilon = 1e-05
highest = lax.Precision.HIGHEST


def passed_along(shard, axis, by):
    length = lax.axis_size(axis)
    pairs = [(i, i + by) for i in range(length) if 0 <= i + by < length]
    return lax.ppermute(shard, axis, pairs)


def prefix(shard, axis, combine, identity):
    length, index = (lax.axis_size(axis), lax.axis_index(axis))
    everything = jax.tree.map(
        lambda part, kind: lax.all_gather(part.astype(kind), axis),
        shard,
        (jnp.bfloat16, jnp.bfloat16),
    )
    start = jax.tree.map(
        lambda part, zero: jnp.broadcast_to(jnp.asarray(zero, part.dtype), part.shape),
        shard,
        identity,
    )

    def prefix_step(k, before):
        reached = k < index
        new = combine(
            before, jax.tree.map(lambda part, own: part[k].astype(own.dtype), everything, shard)
        )
        return jax.tree.map(lambda a, b: jnp.where(reached, a, b), new, before)

    return lax.fori_loop(0, length, prefix_step, start)


def carried_in(shard, axis, combine, identity):
    length, index = (lax.axis_size(axis), lax.axis_index(axis))
    everything = jax.tree.map(
        lambda part, kind: lax.all_gather(part.astype(kind), axis),
        shard,
        jax.tree.map(lambda a: jnp.bfloat16 if a.dtype == jnp.float32 else a.dtype, shard),
    )
    start = jax.tree.map(
        lambda part, zero: jnp.broadcast_to(jnp.asarray(zero, part.dtype), part.shape),
        shard,
        identity,
    )

    def carried_step(k, before):
        at = length - 1 - k
        reached = at > index
        new = combine(
            before, jax.tree.map(lambda part, own: part[at].astype(own.dtype), everything, shard)
        )
        return jax.tree.map(lambda a, b: jnp.where(reached, a, b), new, before)

    return lax.fori_loop(0, length, carried_step, start)


def rms_scale(values, gain):
    return values * lax.rsqrt(jnp.mean(values * values, axis=-1, keepdims=True) + epsilon) * gain


def section_one(projected, rim_rows, conv_weight, conv_bias, step_bias, log_rate):
    tokens = projected.shape[0]
    conv_input = projected[:, DI : DI + XBC]
    step_raw = projected[:, DI + XBC :]
    extended = jnp.concatenate([rim_rows, conv_input], axis=0)
    conv_sum = conv_bias + conv_weight[0] * extended[0:tokens]
    for offset in range(1, CONV):
        conv_sum = conv_sum + conv_weight[offset] * extended[offset : offset + tokens]
    conv_act = jax.nn.silu(conv_sum)
    blocks = tokens // SPAN
    head_input = conv_act[:, :DI].reshape(blocks, SPAN, H, P_SIZE)
    in_coeff = conv_act[:, DI : DI + N].reshape(blocks, SPAN, N)
    out_coeff = conv_act[:, DI + N :].reshape(blocks, SPAN, N)
    step_size = jax.nn.softplus(step_raw + step_bias).reshape(blocks, SPAN, H)
    decays = -jnp.exp(log_rate) * step_size
    inside = jnp.cumsum(decays, axis=1)
    inside_heads = jnp.swapaxes(inside, 1, 2)
    step_heads = jnp.swapaxes(step_size, 1, 2)
    scores = jnp.einsum("ktn,ksn->kts", out_coeff, in_coeff, precision=highest)
    log_gaps = inside_heads[:, :, :, None] - inside_heads[:, :, None, :]
    causal = jnp.arange(SPAN)[:, None] >= jnp.arange(SPAN)[None, :]
    decay_mat = jnp.exp(jnp.where(causal[None, None], log_gaps, -jnp.inf))
    decay_mat = decay_mat * scores[:, None] * step_heads[:, :, None, :]
    inner_out = jnp.einsum("khts,kshp->kthp", decay_mat, head_input, precision=highest)
    last_log = inside[:, -1:, :]
    tail_weight = jnp.exp(last_log - inside) * step_size
    span_state = jnp.einsum(
        "ksh,kshp,ksn->khpn", tail_weight, head_input, in_coeff, precision=highest
    )
    totals = last_log[:, 0, :]

    def carry_step(carry_state, block_item):
        block_total, block_state = block_item
        return (jnp.exp(block_total)[:, None, None] * carry_state + block_state, carry_state)

    final_state, entering = lax.scan(
        carry_step, jnp.zeros((H, P_SIZE, N), jnp.float32), (totals, span_state)
    )
    cross_out = jnp.einsum(
        "kth,ktn,khpn->kthp", jnp.exp(inside), out_coeff, entering, precision=highest
    )
    offsets = jnp.cumsum(totals, axis=0) - totals
    cumulative = (inside + offsets[:, None, :]).reshape(tokens, H)
    ssm_zero = (inner_out + cross_out).reshape(tokens, H, P_SIZE)
    return (
        ssm_zero,
        cumulative,
        out_coeff.reshape(tokens, N),
        head_input.reshape(tokens, H, P_SIZE),
        final_state,
    )


def section_two(
    projected, ssm_zero, cumulative, out_coeff, head_input, state_in, skip_gain, gate_gain
):
    tokens = projected.shape[0]
    gate_part = projected[:, :DI]
    entering = jnp.einsum("tn,hpn->thp", out_coeff, state_in, precision=highest)
    ssm_full = (
        ssm_zero
        + jnp.exp(cumulative)[:, :, None] * entering
        + skip_gain[None, :, None] * head_input
    )
    gated = ssm_full.reshape(tokens, DI) * jax.nn.silu(gate_part)
    return rms_scale(gated, gate_gain)


def join_states(earlier, later):
    return (earlier[0] + later[0], jnp.exp(later[0])[:, None, None] * earlier[1] + later[1])


def join_grads(earlier, later):
    return (earlier[0] + later[0], later[1] + jnp.exp(later[0])[:, None, None] * earlier[1])


def on_device(
    inputs,
    cotangent,
    inproj,
    outproj,
    norm_gain,
    gate_gain,
    conv_weight,
    conv_bias,
    step_bias,
    log_rate,
    skip_gain,
):
    stream = inputs[0].astype(jnp.float32)
    tokens = stream.shape[0]
    rim_start = tokens - CONV + 1
    layer_index = 0
    inproj_full = lax.all_gather(inproj[layer_index], "fsdp", axis=0, tiled=True)
    outproj_full = lax.all_gather(outproj[layer_index], "fsdp", axis=0, tiled=True)
    normed_f, pull_norm = jax.vjp(rms_scale, stream, norm_gain[layer_index])
    normed = normed_f.astype(jnp.bfloat16)
    projected = jnp.dot(normed, inproj_full, preferred_element_type=jnp.float32)
    rim_rows = passed_along(projected[rim_start:, DI : DI + XBC], "seq", 1)
    first_out, pull_first = jax.vjp(
        section_one,
        projected,
        rim_rows,
        conv_weight[layer_index],
        conv_bias[layer_index],
        step_bias[layer_index],
        log_rate[layer_index],
    )
    ssm_zero, cumulative, out_coeff, head_input, final_state = first_out
    total_log = cumulative[tokens - 1]
    entering = prefix(
        (total_log, final_state),
        "seq",
        join_states,
        (jnp.zeros_like(total_log), jnp.zeros_like(final_state)),
    )
    state_in = entering[1]
    mixed_f, pull_second = jax.vjp(
        section_two,
        projected,
        ssm_zero,
        cumulative,
        out_coeff,
        head_input,
        state_in,
        skip_gain[layer_index],
        gate_gain[layer_index],
    )
    mixed_out = mixed_f.astype(jnp.bfloat16)
    stream = stream + jnp.dot(mixed_out, outproj_full, preferred_element_type=jnp.float32)
    stored = [
        (
            inproj_full,
            outproj_full,
            normed,
            mixed_out,
            pull_norm,
            pull_first,
            pull_second,
            total_log,
            state_in,
        )
    ]
    output = stream.astype(jnp.bfloat16)
    grad_stream = cotangent[0].astype(jnp.float32)
    inproj_list = [None] * LAYERS
    outproj_list = [None] * LAYERS
    small_list = [None] * LAYERS
    contract_rows = (((0,), (0,)), ((), ()))
    for layer_index in reversed(range(LAYERS)):
        (
            inproj_full,
            outproj_full,
            normed,
            mixed_out,
            pull_norm,
            pull_first,
            pull_second,
            total_log,
            state_in,
        ) = stored[layer_index]
        out_grad = grad_stream.astype(jnp.bfloat16)
        mix_grad = jnp.dot(out_grad, outproj_full.T, preferred_element_type=jnp.float32)
        second_grads = pull_second(mix_grad)
        (
            proj_second,
            zero_grad,
            cum_part,
            coeff_grad,
            head_grad,
            state_grad,
            skip_part,
            gate_part,
        ) = second_grads
        later = carried_in(
            (total_log, state_grad),
            "seq",
            join_grads,
            (jnp.zeros_like(total_log), jnp.zeros_like(state_grad)),
        )
        later_grad = later[1]
        total_grad = jnp.sum(later_grad * state_in, axis=(1, 2)) * jnp.exp(total_log)
        cum_grad = cum_part.at[tokens - 1].add(total_grad)
        first_grads = pull_first((zero_grad, cum_grad, coeff_grad, head_grad, later_grad))
        proj_first, rim_grad, kernel_part, bias_part, step_part, rate_part = first_grads
        rim_back = passed_along(rim_grad, "seq", -1)
        proj_grad = (proj_first + proj_second).at[rim_start:, DI : DI + XBC].add(rim_back)
        proj_grad_b = proj_grad.astype(jnp.bfloat16)
        normed_grad = jnp.dot(proj_grad_b, inproj_full.T, preferred_element_type=jnp.float32)
        stream_part, norm_part = pull_norm(normed_grad)
        grad_stream = grad_stream + stream_part
        inproj_term = lax.dot_general(
            normed, proj_grad_b, contract_rows, preferred_element_type=jnp.float32
        )
        outproj_term = lax.dot_general(
            mixed_out, out_grad, contract_rows, preferred_element_type=jnp.float32
        )
        inproj_owned, outproj_owned = (
            lax.psum_scatter(
                inproj_term.astype(jnp.bfloat16), "fsdp", scatter_dimension=0, tiled=True
            ).astype(jnp.float32),
            lax.psum_scatter(
                outproj_term.astype(jnp.bfloat16), "fsdp", scatter_dimension=0, tiled=True
            ).astype(jnp.float32),
        )
        inproj_sum, outproj_sum = lax.psum((inproj_owned, outproj_owned), "seq")
        inproj_list[layer_index] = inproj_sum
        outproj_list[layer_index] = outproj_sum
        small_list[layer_index] = (
            norm_part,
            gate_part,
            kernel_part,
            bias_part,
            step_part,
            rate_part,
            skip_part,
        )
    norm_all, gate_all, kernel_all, bias_all, step_all, rate_all, skip_all = [
        jnp.stack([entry[member] for entry in small_list]) for member in range(7)
    ]
    norm_grad, gate_grad, kernel_grad, bias_grad, step_grad, rate_grad, skip_grad = lax.psum(
        (norm_all, gate_all, kernel_all, bias_all, step_all, rate_all, skip_all), ("seq", "fsdp")
    )
    return (
        output[None],
        grad_stream.astype(jnp.bfloat16)[None],
        jnp.stack(inproj_list),
        jnp.stack(outproj_list),
        norm_grad,
        gate_grad,
        kernel_grad,
        bias_grad,
        step_grad,
        rate_grad,
        skip_grad,
    )


def solution(mesh):
    placed = (
        P("fsdp", "seq", None),
        P("fsdp", "seq", None),
        P(None, "fsdp", None),
        P(None, "fsdp", None),
        P(),
        P(),
        P(),
        P(),
        P(),
        P(),
        P(),
    )
    return jax.shard_map(
        on_device,
        mesh=mesh,
        in_specs=placed,
        out_specs=(
            P("fsdp", "seq", None),
            P("fsdp", "seq", None),
            P(None, "fsdp", None),
            P(None, "fsdp", None),
            P(),
            P(),
            P(),
            P(),
            P(),
            P(),
            P(),
        ),
        check_vma=False,
    )
```

profile of v0, /device:TPU:0, one launch (start us, length us, event | category | flops | bytes accessed | tf_op | source)
XLA Modules:
  0.0 550.7 jit_solution(2837934593614807210)
XLA Ops:
  12.7 40.4 %all-gather.10.cloned.1.call-done = bf16[1,768,3352]{2,1,0:T(8,128)(2,1)} async-done(((bf16[1,192,3352]{2,1,0:T(8,128)(2,1)}), bf16[1,768,3352]{2,1,0:T(8,128)(2,1)}) %all-gather.10.cloned.1.call-update) | async-done | bytes 5148688 | tf_op jit(solution)/shard_map/all_gather | solution.py:168
  53.1 4.7 fusion.8
  61.1 3.5 collective-permute-start
  67.7 5.5 fusion.74
  79.3 5.0 fusion.37
  84.5 4.3 while.68
  99.8 21.7 %all-gather.4 = bf16[8,1,24]{2,1,0:T(2,128)(2,1)S(1)} all-gather(bf16[1,1,24]{2,1,0:T(2,128)(2,1)} %bitcast.264), channel_id=1, replica_groups=mesh['seq'=8,'fsdp'=4] {'seq'}, dimensions={0}, use_global_device_ids=true | all-gather | bytes 432 | tf_op jit(solution)/shard_map/all_gather | solution.py:27
  127.3 3.2 fusion.22
  133.5 17.1 %all-gather.12.cloned.1.call-done = bf16[192,64,128]{2,1,0:T(8,128)(2,1)} async-done(((bf16[24,64,128]{2,1,0:T(8,128)(2,1)}), bf16[192,64,128]{2,1,0:T(8,128)(2,1)}) %all-gather.12.cloned.1.call-update) | async-done | bytes 3145744 | tf_op jit(solution)/shard_map/all_gather | solution.py:27
  150.6 15.3 %while.69 = (s32[]{:T(128)}, f32[24,64,128]{2,1,0:T(8,128)S(1)}, s32[]{:T(128)}, bf16[8,24]{1,0:T(8,128)(2,1)}, bf16[8,24,64,128]{3,2,1,0:T(8,128)(2,1)}, /*index=5*/s32[]{:T(128)}, s32[]{:T(128)}) while((s32[]{:T(128)}, f32[24,64,128]{2,1,0:T(8,128)S(1)}, s32[]{:T(128)}, bf16[8,24]{1,0:T(8,128)(2,1)}, ...), condition=%wide.region_6.7_spmd.clone, body=%wide.region_5.6_spmd.clone.sunk | while | flops 983068 | bytes 1966433 | solution.py:44
  170.3 4.6 all-gather.14.cloned.1.call-done
  174.9 3.3 multiply_reduce_fusion.8
  187.7 3.4 fusion.59
  194.0 4.2 fusion.69
  208.2 35.0 %all-gather.16.cloned.1.call-done = bf16[192,64,128]{2,1,0:T(8,128)(2,1)} async-done(((bf16[24,64,128]{2,1,0:T(8,128)(2,1)}), bf16[192,64,128]{2,1,0:T(8,128)(2,1)}) %all-gather.16.cloned.1.call-update) | async-done | bytes 3145744 | tf_op jit(solution)/shard_map/all_gather | solution.py:50
  243.2 15.4 %while.70 = (s32[]{:T(128)}, f32[24,64,128]{2,1,0:T(8,128)S(1)}, s32[]{:T(128)}, bf16[8,24,64,128]{3,2,1,0:T(8,128)(2,1)}, bf16[8,24]{1,0:T(8,128)(2,1)}, /*index=5*/s32[]{:T(128)}, s32[]{:T(128)}, s32[]{:T(128)}, s32[]{:T(128)}) while((s32[]{:T(128)}, f32[24,64,128]{2,1,0:T(8,128)S(1)}, s32[]{:T(128)}, ...), condition=%wide.region_10.11_spmd.clone, body=%wide.region_9.10_spmd.clone.sunk | while | flops 983072 | bytes 1966495 | solution.py:68
  262.1 6.6 %while.67 = (s32[]{:T(128)}, f32[24,64,128]{2,1,0:T(8,128)S(1)}, f32[2,24]{1,0:T(2,128)S(1)}, f32[2,24,64,128]{3,2,1,0:T(8,128)}, f32[2,24,64,128]{3,2,1,0:T(8,1...) while((s32[]{:T(128)}, f32[24,64,128]{2,1,0:T(8,128)S(1)}, ...), condition=%wide.region_13.14_spmd, body=%wide.region_11.13_spmd.sunk | while | flops 786435 | bytes 11011073 | solution.py:110
  269.2 3.9 fusion.56
  273.2 4.6 fusion.142
  277.9 4.8 bitcast_add_fusion.2
  283.6 3.8 copy.420
  293.5 6.2 %multiply_reduce_fusion.5 = (f32[1792]{0:T(1024)}, f32[1792]{0:T(1024)}, f32[1792]{0:T(1024)}, f32[1792]{0:T(1024)}, f32[1792]{0:T(1024)}, /*index=5*/f32[128,1792]{0,1:T(8,128)S(1)}) fusion(f32[128,1792]{0,1:T(8,128)} %slice.113, f32[3,1792]{0,1:T(8,128)} %copy.364, f32[128,3352]{0,1:T(8,128)S(1)} %copy-done.10, f32[128,1792]{0,1:T(8,128)} %get-tuple-element.620, ...), kind=kLoop, calls=%fused_computation.93 | loop fusion | flops 5266688 | bytes 4644864 | tf_op jit(solution)/shard_map/transpose(jvp())/reduce_sum | solution.py:82
  305.7 3.1 multiply_reduce_fusion
  322.5 8.7 %scatter-add.9 = f32[128,3352]{0,1:T(8,128)S(1)} dynamic-update-slice(f32[128,3352]{0,1:T(8,128)S(1)} %pad_add_fusion.1, f32[3,1792]{0,1:T(8,128)S(1)} %slice_add_fusion, s32[]{:T(128)} %constant.233.clone.1, s32[]{:T(128)} %constant.234.clone.1) | dynamic-update-slice | bytes 43012 | tf_op jit(solution)/shard_map/scatter-add | solution.py:261
  331.3 4.0 convolution_convert_fusion
  337.5 49.3 %reduce-scatter.3.cloned.1.call-done = bf16[192,3352]{1,0:T(8,128)(2,1)} async-done(((bf16[768,3352]{1,0:T(8,128)(2,1)}), bf16[192,3352]{1,0:T(8,128)(2,1)}) %reduce-scatter.3.cloned.1.call-update) | async-done | bytes 1287184 | tf_op jit(solution)/shard_map/reduce_scatter | solution.py:273
  386.8 3.0 bitcast_convert_fusion
  391.1 3.1 fusion.53
  394.4 4.8 fusion.102
  399.2 44.4 %all-reduce.15 = (f32[1,768]{1,0:T(1,128)}, f32[1,1536]{1,0:T(1,128)}, f32[1,4,1792]{2,1,0:T(4,128)}, f32[1,1792]{1,0:T(1,128)}, f32[1,24]{1,0:T(1,128)}, /*index=5*/f32[1,24]{1,0:T(1,128)}, f32[1,24]{1,0:T(1,128)}) all-reduce(f32[1,768]{1,0:T(1,128)S(1)} %reshape.359, ...), channel_id=1, replica_groups=mesh['seq'=8,'fsdp'=4] {'seq','fsdp'}, use_global_device_ids=true, to_apply=%region_30.31 | all-reduce | flops 11336 | bytes 90688 | tf_op jit(solution)/shard_map/psum | solution.py:295
  444.5 94.6 %all-reduce.19.cloned.1.call-done = (f32[1,192,3352]{2,1,0:T(8,128)}, f32[1,384,768]{2,1,0:T(8,128)}) async-done(((f32[1,192,3352]{2,1,0:T(8,128)}, f32[1,384,768]{2,1,0:T(8,128)}), (f32[1,192,3352]{2,1,0:T(8,128)}, f32[1,384,768]{2,1,0:T(8,128)})) %all-reduce.19.cloned.1.call-update) | async-done | bytes 3754000 | tf_op jit(solution)/shard_map/psum | solution.py:280
  539.1 3.5 copy.534
  (416 shorter events, 141.0 us)
Async XLA Ops:
  7.2 45.9 %copy-start.21 = (bf16[1,128,768]{2,1,0:T(8,128)(2,1)S(1)}, bf16[1,128,768]{2,1,0:T(8,128)(2,1)}, u32[]{:S(2)}) copy-start(bf16[1,128,768]{2,1,0:T(8,128)(2,1)} %param.23) | copy-start | bytes 589828
  7.2 45.9 %all-gather.10.cloned.1.call-start = ((), (), s32[]{:S(2)}) async-start(), calls=%async_computation.4 | async-start | bytes 6635520 | tf_op jit(solution)/shard_map/all_gather | solution.py:168
  7.9 142.7 %all-gather.12.cloned.1.call-start = ((), (), s32[]{:S(2)}) async-start(), calls=%async_computation.5 | async-start | bytes 3538944 | tf_op jit(solution)/shard_map/all_gather | solution.py:27
  11.6 56.0 %copy-start.67 = (f32[1792]{0:T(1024)}, f32[1792]{0:T(1024)S(1)}, u32[]{:S(2)}) copy-start(f32[1792]{0:T(1024)S(1)} %get-tuple-element.543) | copy-start | bytes 21508
  12.7 45.1 %copy-start.107 = (f32[128]{0:T(128)}, f32[128]{0:T(128)S(1)}, u32[]{:S(2)}) copy-start(f32[128]{0:T(128)S(1)} %fusion.105) | copy-start | bytes 1540
  12.7 45.3 %copy-start.98 = (f32[24]{0:T(128)}, f32[24]{0:T(128)S(1)}, u32[]{:S(2)}) copy-start(f32[24]{0:T(128)S(1)} %negate_bitcast_fusion) | copy-start | bytes 292
  12.7 45.1 %copy-start.91 = (f32[128]{0:T(128)}, f32[128]{0:T(128)S(1)}, u32[]{:S(2)}) copy-start(f32[128]{0:T(128)S(1)} %fusion.124) | copy-start | bytes 1540
  12.7 45.1 %copy-start.101 = (f32[1,24]{1,0:T(1,128)S(1)}, f32[1,24]{1,0:T(1,128)}, u32[]{:S(2)}) copy-start(f32[1,24]{1,0:T(1,128)} %param.31) | copy-start | bytes 292
  57.8 7.5 %copy-start.8 = (f32[128,3352]{0,1:T(8,128)}, f32[128,3352]{0,1:T(8,128)S(1)}, u32[]{:S(2)}) copy-start(f32[128,3352]{0,1:T(8,128)S(1)} %fusion.8) | copy-start | bytes 5148676
  58.0 6.6 %copy-start.40 = (f32[2,64,24]{1,0,2:T(2,128)}, f32[2,64,24]{1,0,2:T(2,128)S(1)}, u32[]{:S(2)}) copy-start(f32[2,64,24]{1,0,2:T(2,128)S(1)} %reshape.346) | copy-start | bytes 36868
  58.3 8.0 %copy-start.37 = (f32[2,64,24]{2,1,0:T(8,128)}, f32[2,64,24]{2,1,0:T(8,128)S(1)}, u32[]{:S(2)}) copy-start(f32[2,64,24]{2,1,0:T(8,128)S(1)} %reduce_window_sum.46) | copy-start | bytes 36868
  58.4 7.9 %copy-start.42 = (f32[2,64,24]{1,2,0:T(8,128)}, f32[2,64,24]{1,2,0:T(8,128)S(1)}, u32[]{:S(2)}) copy-start(f32[2,64,24]{1,2,0:T(8,128)S(1)} %copy.373) | copy-start | bytes 36868
  61.1 6.5 %copy-start.69 = (f32[1792]{0:T(1024)S(1)}, f32[1792]{0:T(1024)}, u32[]{:S(2)}) copy-start(f32[1792]{0:T(1024)} %get-tuple-element.544) | copy-start | bytes 21508
  61.1 6.5 %copy-start.71 = (f32[1792]{0:T(1024)S(1)}, f32[1792]{0:T(1024)}, u32[]{:S(2)}) copy-start(f32[1792]{0:T(1024)} %get-tuple-element.545) | copy-start | bytes 21508
  61.1 6.5 %copy-start.73 = (f32[1792]{0:T(1024)S(1)}, f32[1792]{0:T(1024)}, u32[]{:S(2)}) copy-start(f32[1792]{0:T(1024)} %get-tuple-element.546) | copy-start | bytes 21508
  61.1 6.5 %copy-start.87 = (f32[1792]{0:T(1024)S(1)}, f32[1792]{0:T(1024)}, u32[]{:S(2)}) copy-start(f32[1792]{0:T(1024)} %reduce.9) | copy-start | bytes 21508
  61.1 5.2 collective-permute-start
  73.1 92.8 %copy-start.22 = (f32[128,1792]{0,1:T(8,128)}, f32[128,1792]{0,1:T(8,128)S(1)}, u32[]{:S(2)}) copy-start(f32[128,1792]{0,1:T(8,128)S(1)} %get-tuple-element.619) | copy-start | bytes 2752516
  88.8 38.4 %copy-start = (f32[2,24,64,128]{3,2,1,0:T(8,128)}, f32[2,24,64,128]{3,2,1,0:T(8,128)S(1)}, u32[]{:S(2)}) copy-start(f32[2,24,64,128]{3,2,1,0:T(8,128)S(1)} %get-tuple-element.878) | copy-start | bytes 4718596
  89.7 85.2 %all-gather.14.cloned.1.call-start = ((), (), s32[]{:S(2)}) async-start(), calls=%async_computation.6 | async-start | bytes 2949120 | tf_op jit(solution)/shard_map/all_gather | solution.py:169
  90.5 152.8 %all-gather.16.cloned.1.call-start = ((), (), s32[]{:S(2)}) async-start(), calls=%async_computation.7 | async-start | bytes 3538944 | tf_op jit(solution)/shard_map/all_gather | solution.py:50
  95.6 31.5 %copy-start.54 = (f32[128,24]{0,1:T(8,128)}, f32[128,24]{0,1:T(8,128)S(1)}, u32[]{:S(2)}) copy-start(f32[128,24]{0,1:T(8,128)S(1)} %copy.379) | copy-start | bytes 36868
  169.3 8.9 %copy-start.11 = (f32[128,1536]{0,1:T(8,128)}, f32[128,1536]{0,1:T(8,128)S(1)}, u32[]{:S(2)}) copy-start(f32[128,1536]{0,1:T(8,128)S(1)} %get-tuple-element.618) | copy-start | bytes 2359300
  183.0 152.3 %reduce-scatter.5.cloned.1.call-start = ((), (), s32[]{:S(2)}) async-start(), calls=%async_computation.3 | async-start | bytes 2949120 | tf_op jit(solution)/shard_map/reduce_scatter | solution.py:276
  207.7 179.1 %reduce-scatter.3.cloned.1.call-start = ((), (), s32[]{:S(2)}) async-start(), calls=%async_computation.2 | async-start | bytes 6635520 | tf_op jit(solution)/shard_map/reduce_scatter | solution.py:273
  262.1 7.2 %copy-start.47 = (f32[2,64,24]{1,2,0:T(8,128)S(1)}, f32[2,64,24]{1,2,0:T(8,128)}, u32[]{:S(2)}) copy-start(f32[2,64,24]{1,2,0:T(8,128)} %get-tuple-element.631) | copy-start | bytes 36868
  293.5 6.3 %copy-start.70 = (f32[1792]{0:T(1024)S(1)}, f32[1792]{0:T(1024)}, u32[]{:S(2)}) copy-start(f32[1792]{0:T(1024)} %get-tuple-element.544) | copy-start | bytes 21508
  312.9 6.1 %collective-permute-start.1 = (f32[3,1792]{1,0:T(4,128)}, f32[3,1792]{1,0:T(4,128)}, u32[]{:S(2)}, u32[]{:S(2)}) collective-permute-start(f32[3,1792]{1,0:T(4,128)} %copy.407), channel_id=1, source_target_pairs={{4,0},{8,4},{12,8},{16,12},{20,16},{24,20},{28,24},{5,1},{9,5},{13... | collective-permute-start | bytes 64520 | tf_op jit(solution)/shard_map/ppermute | solution.py:21
  322.5 8.7 %copy-start.92 = (f32[128]{0:T(128)S(1)}, f32[128]{0:T(128)}, u32[]{:S(2)}) copy-start(f32[128]{0:T(128)} %copy-done.91) | copy-start | bytes 1540
  335.3 203.8 %all-reduce.19.cloned.1.call-start = ((), (), s32[]{:S(2)}) async-start(), calls=%async_computation.8 | async-start | bytes 7667712 | tf_op jit(solution)/shard_map/psum | solution.py:280
  394.4 49.2 %copy-start.108 = (f32[128]{0:T(128)S(1)}, f32[128]{0:T(128)}, u32[]{:S(2)}) copy-start(f32[128]{0:T(128)} %copy-done.107) | copy-start | bytes 1540
  394.4 49.2 %copy-start.34 = (bf16[1,128,768]{2,1,0:T(8,128)(2,1)S(1)}, bf16[1,128,768]{2,1,0:T(8,128)(2,1)}, u32[]{:S(2)}) copy-start(bf16[1,128,768]{2,1,0:T(8,128)(2,1)} %param.24) | copy-start | bytes 589828
  (94 other events, 282.8 us)
Sparse Core Ops, SparseCore 0:
  9.6 43.4 all-gather.9
  89.8 60.7 all-gather.11
  152.2 22.6 all-gather.13
  183.1 60.0 all-gather.15
  246.2 31.4 reduce-scatter.4
  335.4 51.3 reduce-scatter.2
  391.1 147.9 all-reduce.18
where the time goes:
time: 560 us; the launch traced here: 551 us
  waiting for transfers between devices  245 us (44%)
  other arithmetic  78.2 us (14%)
  local copies, waits for them, and re-layouts  75.6 us (13%)
  blocking collectives  66.1 us (12%)
  matrix products  63.5 us (11%)
  between operations  15.7 us (3%)
  starting transfers between devices  5.68 us (1%)
    psum x1, waiting for transfers between devices, on_device(): inproj_sum, outproj_sum = lax.psum((inproj_owned, outproj_owned), 'seq')  94.6 us
    reduce_scatter x1, waiting for transfers between devices, on_device(): lax.psum_scatter(inproj_term.astype(jnp.bfloat16), 'fsdp', scatter_dimens...  49.3 us
    psum x1, blocking collectives, on_device(): lax.psum((norm_all, gate_all, kernel_all, bias_all, step_all, rate_all, s...  44.4 us
    all_gather x1, waiting for transfers between devices, on_device(): lax.all_gather(inproj[layer_index], 'fsdp', axis=0, tiled=True)  40.4 us
    all_gather x1, waiting for transfers between devices, carried_in(): lax.all_gather(part.astype(kind), axis)  35 us
    all_gather x1, blocking collectives, prefix(): lax.all_gather(part.astype(kind), axis)  21.7 us
    unnamed x231, local copies, waits for them, and re-layouts  17.7 us
    all_gather x1, waiting for transfers between devices, prefix(): lax.all_gather(part.astype(kind), axis)  17.1 us
  transfers between devices with their start and end apart: 9, of which 7 were waited for; matrix products, arithmetic and copies ran while one was open for 30% of the time, Pallas kernels for 0%

commit v1 on v0

--- a/solution.py
+++ b/solution.py
@@ -165,7 +165,20 @@
     tokens = stream.shape[0]
     rim_start = tokens - CONV + 1
     layer_index = 0
-    inproj_full = lax.all_gather(inproj[layer_index], "fsdp", axis=0, tiled=True)
+
+    def link_keys(dev_axis, field_in, in_dim):
+        axis_total = jax.lax.axis_size(dev_axis)
+        steps_seen = tuple(((i0, (i0 + 1) % axis_total) for i0 in range(axis_total)))
+        prior = [None] * axis_total
+        prior[axis_total - 1] = field_in
+        for idx in range(axis_total - 2, -1, -1):
+            prior[idx] = jax.lax.ppermute(prior[idx + 1], axis_name=dev_axis, perm=steps_seen)
+        lower = jnp.concatenate(prior, in_dim)
+        carry = (jax.lax.axis_index(dev_axis) + 1) * field_in.shape[in_dim]
+        big = jnp.roll(lower, carry, in_dim)
+        return big
+
+    inproj_full = link_keys("fsdp", inproj[layer_index], 0)
     outproj_full = lax.all_gather(outproj[layer_index], "fsdp", axis=0, tiled=True)
     normed_f, pull_norm = jax.vjp(rms_scale, stream, norm_gain[layer_index])
     normed = normed_f.astype(jnp.bfloat16)

time: 560 us -> 578 us (1.032)
  local copies, waits for them, and re-layouts: 75.6 us -> 84.9 us
  waiting for transfers between devices: 245 us -> 252 us
    ppermute x0 -> x3, waiting for transfers between devices: none -> 46.7 us  [link_keys(): jax.lax.ppermute(prior[idx + 1], axis_name=dev_axis, perm=steps_seen)]
    all_gather x1 -> x0, waiting for transfers between devices: 40.4 us -> none  [on_device(): lax.all_gather(inproj[layer_index], 'fsdp', axis=0, tiled=True)]
    unnamed x231 -> x244, local copies, waits for them, and re-layouts: 17.7 us -> 26.8 us
  transfers between devices with their start and end apart: 9 -> 11, of which waited for: 7 -> 9; matrix products, arithmetic and copies ran while one was open for 30% -> 29% of each run, Pallas kernels for 0% -> 0%
where the time goes in v1:
time: 578 us; the launch traced here: 567 us
  waiting for transfers between devices  252 us (44%)
  local copies, waits for them, and re-layouts  84.9 us (15%)
  other arithmetic  79 us (14%)
  blocking collectives  65.9 us (11%)
  matrix products  61.4 us (11%)
  between operations  15.8 us (3%)
  starting transfers between devices  7.1 us (1%)
    psum x1, waiting for transfers between devices, on_device(): inproj_sum, outproj_sum = lax.psum((inproj_owned, outproj_owned), 'seq')  94.6 us
    reduce_scatter x1, waiting for transfers between devices, on_device(): lax.psum_scatter(inproj_term.astype(jnp.bfloat16), 'fsdp', scatter_dimens...  49.3 us
    ppermute x3, waiting for transfers between devices, link_keys(): jax.lax.ppermute(prior[idx + 1], axis_name=dev_axis, perm=steps_seen)  46.7 us
    psum x1, blocking collectives, on_device(): lax.psum((norm_all, gate_all, kernel_all, bias_all, step_all, rate_all, s...  44 us
    all_gather x1, waiting for transfers between devices, carried_in(): lax.all_gather(part.astype(kind), axis)  35.2 us
    unnamed x244, local copies, waits for them, and re-layouts  26.8 us
    all_gather x1, blocking collectives, prefix(): lax.all_gather(part.astype(kind), axis)  21.9 us
    all_gather x1, waiting for transfers between devices, prefix(): lax.all_gather(part.astype(kind), axis)  18.2 us
  transfers between devices with their start and end apart: 11, of which 9 were waited for; matrix products, arithmetic and copies ran while one was open for 29% of the time, Pallas kernels for 0%

profile of v1, /device:TPU:0, one launch (start us, length us, event | category | flops | bytes accessed | tf_op | source)
XLA Modules:
  0.0 566.7 jit_solution(10062592755605365082)
XLA Ops:
  7.8 17.6 %collective-permute-done = bf16[192,3352]{1,0:T(8,128)(2,1)S(1)} collective-permute-done((bf16[192,3352]{1,0:T(8,128)(2,1)}, bf16[192,3352]{1,0:T(8,128)(2,1)S(1)}, u32[]{:S(2)}, u32[]{:S(2)}) %collective-permute-start) | collective-permute-done | bytes 1287200 | tf_op jit(solution)/shard_map/ppermute | solution.py:175
  25.4 17.2 %collective-permute-done.1 = bf16[192,3352]{1,0:T(8,128)(2,1)S(1)} collective-permute-done((bf16[192,3352]{1,0:T(8,128)(2,1)S(1)}, bf16[192,3352]{1,0:T(8,128)(2,1)S(1)}, u32[]{:S(2)}, u32[]{:S(2)}) %collective-permute-start.1) | collective-permute-done | bytes 1287200 | tf_op jit(solution)/shard_map/ppermute | solution.py:175
  48.0 11.9 %collective-permute-done.2 = bf16[192,3352]{1,0:T(8,128)(2,1)} collective-permute-done((bf16[192,3352]{1,0:T(8,128)(2,1)S(1)}, bf16[192,3352]{1,0:T(8,128)(2,1)}, u32[]{:S(2)}, u32[]{:S(2)}) %collective-permute-start.2) | collective-permute-done | bytes 1287200 | tf_op jit(solution)/shard_map/ppermute | solution.py:175
  65.3 4.0 copy-done.20
  75.2 4.3 collective-permute-start.3
  82.5 5.4 fusion.74
  94.1 5.0 fusion.37
  99.2 4.3 while.68
  114.6 21.9 %all-gather.3 = bf16[8,1,24]{2,1,0:T(2,128)(2,1)S(1)} all-gather(bf16[1,1,24]{2,1,0:T(2,128)(2,1)} %bitcast.261), channel_id=1, replica_groups=mesh['seq'=8,'fsdp'=4] {'seq'}, dimensions={0}, use_global_device_ids=true | all-gather | bytes 432 | tf_op jit(solution)/shard_map/all_gather | solution.py:27
  142.3 3.2 fusion.22
  148.4 18.2 %all-gather.8.cloned.1.call-done = bf16[192,64,128]{2,1,0:T(8,128)(2,1)} async-done(((bf16[24,64,128]{2,1,0:T(8,128)(2,1)}), bf16[192,64,128]{2,1,0:T(8,128)(2,1)}) %all-gather.8.cloned.1.call-update) | async-done | bytes 3145744 | tf_op jit(solution)/shard_map/all_gather | solution.py:27
  166.6 15.2 %while.69 = (s32[]{:T(128)}, f32[24,64,128]{2,1,0:T(8,128)S(1)}, s32[]{:T(128)}, bf16[8,24]{1,0:T(8,128)(2,1)}, bf16[8,24,64,128]{3,2,1,0:T(8,128)(2,1)}, /*index=5*/s32[]{:T(128)}, s32[]{:T(128)}) while((s32[]{:T(128)}, f32[24,64,128]{2,1,0:T(8,128)S(1)}, s32[]{:T(128)}, bf16[8,24]{1,0:T(8,128)(2,1)}, ...), condition=%wide.region_6.7_spmd.clone, body=%wide.region_5.6_spmd.clone.sunk | while | flops 983068 | bytes 1966433 | solution.py:44
  186.3 4.6 all-gather.10.cloned.1.call-done
  190.9 3.3 multiply_reduce_fusion.8
  203.6 3.4 fusion.59
  209.9 4.2 fusion.69
  224.0 35.2 %all-gather.12.cloned.1.call-done = bf16[192,64,128]{2,1,0:T(8,128)(2,1)} async-done(((bf16[24,64,128]{2,1,0:T(8,128)(2,1)}), bf16[192,64,128]{2,1,0:T(8,128)(2,1)}) %all-gather.12.cloned.1.call-update) | async-done | bytes 3145744 | tf_op jit(solution)/shard_map/all_gather | solution.py:50
  259.2 15.4 %while.70 = (s32[]{:T(128)}, f32[24,64,128]{2,1,0:T(8,128)S(1)}, s32[]{:T(128)}, bf16[8,24,64,128]{3,2,1,0:T(8,128)(2,1)}, bf16[8,24]{1,0:T(8,128)(2,1)}, /*index=5*/s32[]{:T(128)}, s32[]{:T(128)}, s32[]{:T(128)}, s32[]{:T(128)}) while((s32[]{:T(128)}, f32[24,64,128]{2,1,0:T(8,128)S(1)}, s32[]{:T(128)}, ...), condition=%wide.region_10.11_spmd.clone, body=%wide.region_9.10_spmd.clone.sunk | while | flops 983072 | bytes 1966495 | solution.py:68
  278.1 6.6 %while.67 = (s32[]{:T(128)}, f32[24,64,128]{2,1,0:T(8,128)S(1)}, f32[2,24]{1,0:T(2,128)S(1)}, f32[2,24,64,128]{3,2,1,0:T(8,128)}, f32[2,24,64,128]{3,2,1,0:T(8,1...) while((s32[]{:T(128)}, f32[24,64,128]{2,1,0:T(8,128)S(1)}, ...), condition=%wide.region_13.14_spmd, body=%wide.region_11.13_spmd.sunk | while | flops 786435 | bytes 11011073 | solution.py:110
  285.2 3.9 fusion.56
  289.2 4.6 fusion.144
  293.9 4.8 bitcast_add_fusion.2
  299.6 3.8 copy.420
  309.6 6.5 %multiply_reduce_fusion.5 = (f32[1792]{0:T(1024)}, f32[1792]{0:T(1024)}, f32[1792]{0:T(1024)}, f32[1792]{0:T(1024)}, f32[1792]{0:T(1024)}, /*index=5*/f32[128,1792]{0,1:T(8,128)S(1)}) fusion(f32[128,1792]{0,1:T(8,128)} %slice.113, f32[3,1792]{0,1:T(8,128)} %copy.364, f32[128,3352]{0,1:T(8,128)S(1)} %copy-done.10, f32[128,1792]{0,1:T(8,128)} %get-tuple-element.620, ...), kind=kLoop, calls=%fused_computation.93 | loop fusion | flops 5266688 | bytes 4644864 | tf_op jit(solution)/shard_map/transpose(jvp())/reduce_sum | solution.py:82
  338.8 8.7 %scatter-add.9 = f32[128,3352]{0,1:T(8,128)S(1)} dynamic-update-slice(f32[128,3352]{0,1:T(8,128)S(1)} %pad_add_fusion.1, f32[3,1792]{0,1:T(8,128)S(1)} %slice_add_fusion, s32[]{:T(128)} %constant.258.clone.1, s32[]{:T(128)} %constant.259.clone.1) | dynamic-update-slice | bytes 43012 | tf_op jit(solution)/shard_map/scatter-add | solution.py:274
  347.5 4.0 convolution_convert_fusion
  353.8 49.3 %reduce-scatter.3.cloned.1.call-done = bf16[192,3352]{1,0:T(8,128)(2,1)} async-done(((bf16[768,3352]{1,0:T(8,128)(2,1)}), bf16[192,3352]{1,0:T(8,128)(2,1)}) %reduce-scatter.3.cloned.1.call-update) | async-done | bytes 1287184 | tf_op jit(solution)/shard_map/reduce_scatter | solution.py:286
  407.3 3.1 fusion.53
  410.7 5.0 fusion.102
  415.7 44.0 %all-reduce.15 = (f32[1,768]{1,0:T(1,128)}, f32[1,1536]{1,0:T(1,128)}, f32[1,4,1792]{2,1,0:T(4,128)}, f32[1,1792]{1,0:T(1,128)}, f32[1,24]{1,0:T(1,128)}, /*index=5*/f32[1,24]{1,0:T(1,128)}, f32[1,24]{1,0:T(1,128)}) all-reduce(f32[1,768]{1,0:T(1,128)S(1)} %reshape.359, ...), channel_id=1, replica_groups=mesh['seq'=8,'fsdp'=4] {'seq','fsdp'}, use_global_device_ids=true, to_apply=%region_30.31 | all-reduce | flops 11336 | bytes 90688 | tf_op jit(solution)/shard_map/psum | solution.py:308
  460.5 94.6 %all-reduce.19.cloned.1.call-done = (f32[1,192,3352]{2,1,0:T(8,128)}, f32[1,384,768]{2,1,0:T(8,128)}) async-done(((f32[1,192,3352]{2,1,0:T(8,128)}, f32[1,384,768]{2,1,0:T(8,128)}), (f32[1,192,3352]{2,1,0:T(8,128)}, f32[1,384,768]{2,1,0:T(8,128)})) %all-reduce.19.cloned.1.call-update) | async-done | bytes 3754000 | tf_op jit(solution)/shard_map/psum | solution.py:293
  555.1 3.5 copy.541
  (433 shorter events, 155.3 us)
Async XLA Ops:
  7.2 159.4 %all-gather.8.cloned.1.call-start = ((), (), s32[]{:S(2)}) async-start(), calls=%async_computation.4 | async-start | bytes 3538944 | tf_op jit(solution)/shard_map/all_gather | solution.py:27
  7.2 18.2 %collective-permute-start = (bf16[192,3352]{1,0:T(8,128)(2,1)}, bf16[192,3352]{1,0:T(8,128)(2,1)S(1)}, u32[]{:S(2)}, u32[]{:S(2)}) collective-permute-start(bf16[192,3352]{1,0:T(8,128)(2,1)} %bitcast.234), channel_id=1, source_target_pairs={{0,1},{1,2},{2,3},{3,0},{4,5},{5,6},{6,7},{7,4},{8,9},{9,10},{10,1... | collective-permute-start | bytes 3861512 | tf_op jit(solution)/shard_map/ppermute | solution.py:175
  25.4 17.2 %collective-permute-start.1 = (bf16[192,3352]{1,0:T(8,128)(2,1)S(1)}, bf16[192,3352]{1,0:T(8,128)(2,1)S(1)}, u32[]{:S(2)}, u32[]{:S(2)}) collective-permute-start(bf16[192,3352]{1,0:T(8,128)(2,1)S(1)} %collective-permute-done), channel_id=1, source_target_pairs={{0,1},{1,2},{2,3},{3,0},{4,5},{5,6},{6,7},{7,4},{8,9},{9,10},{10,1... | collective-permute-start | bytes 3861512 | tf_op jit(solution)/shard_map/ppermute | solution.py:175
  42.6 18.7 %copy-start.33 = (bf16[192,3352]{1,0:T(8,128)(2,1)}, bf16[192,3352]{1,0:T(8,128)(2,1)S(1)}, u32[]{:S(2)}) copy-start(bf16[192,3352]{1,0:T(8,128)(2,1)S(1)} %collective-permute-done.1) | copy-start | bytes 3861508
  42.6 17.3 %collective-permute-start.2 = (bf16[192,3352]{1,0:T(8,128)(2,1)S(1)}, bf16[192,3352]{1,0:T(8,128)(2,1)}, u32[]{:S(2)}, u32[]{:S(2)}) collective-permute-start(bf16[192,3352]{1,0:T(8,128)(2,1)S(1)} %collective-permute-done.1), channel_id=1, source_target_pairs={{0,1},{1,2},{2,3},{3,0},{4,5},{5,6},{6,7},{7,4},{8,9},{9,10},{10,1... | collective-permute-start | bytes 3861512 | tf_op jit(solution)/shard_map/ppermute | solution.py:175
  47.3 14.2 %copy-start.111 = (f32[128]{0:T(128)}, f32[128]{0:T(128)S(1)}, u32[]{:S(2)}) copy-start(f32[128]{0:T(128)S(1)} %fusion.105) | copy-start | bytes 1540
  47.9 24.1 %copy-start.102 = (f32[24]{0:T(128)}, f32[24]{0:T(128)S(1)}, u32[]{:S(2)}) copy-start(f32[24]{0:T(128)S(1)} %negate_bitcast_fusion) | copy-start | bytes 292
  48.0 17.3 %copy-start.95 = (f32[128]{0:T(128)}, f32[128]{0:T(128)S(1)}, u32[]{:S(2)}) copy-start(f32[128]{0:T(128)S(1)} %fusion.126) | copy-start | bytes 1540
  71.9 8.3 %copy-start.8 = (f32[128,3352]{0,1:T(8,128)}, f32[128,3352]{0,1:T(8,128)S(1)}, u32[]{:S(2)}) copy-start(f32[128,3352]{0,1:T(8,128)S(1)} %fusion.8) | copy-start | bytes 5148676
  72.1 7.4 %copy-start.44 = (f32[2,64,24]{1,0,2:T(2,128)}, f32[2,64,24]{1,0,2:T(2,128)S(1)}, u32[]{:S(2)}) copy-start(f32[2,64,24]{1,0,2:T(2,128)S(1)} %reshape.346) | copy-start | bytes 36868
  72.3 8.8 %copy-start.41 = (f32[2,64,24]{2,1,0:T(8,128)}, f32[2,64,24]{2,1,0:T(8,128)S(1)}, u32[]{:S(2)}) copy-start(f32[2,64,24]{2,1,0:T(8,128)S(1)} %reduce_window_sum.46) | copy-start | bytes 36868
  72.4 8.7 %copy-start.46 = (f32[2,64,24]{1,2,0:T(8,128)}, f32[2,64,24]{1,2,0:T(8,128)S(1)}, u32[]{:S(2)}) copy-start(f32[2,64,24]{1,2,0:T(8,128)S(1)} %copy.373) | copy-start | bytes 36868
  75.1 7.3 %copy-start.71 = (f32[1792]{0:T(1024)S(1)}, f32[1792]{0:T(1024)}, u32[]{:S(2)}) copy-start(f32[1792]{0:T(1024)} %get-tuple-element.543) | copy-start | bytes 21508
  75.1 7.3 %copy-start.73 = (f32[1792]{0:T(1024)S(1)}, f32[1792]{0:T(1024)}, u32[]{:S(2)}) copy-start(f32[1792]{0:T(1024)} %get-tuple-element.544) | copy-start | bytes 21508
  75.1 7.3 %copy-start.75 = (f32[1792]{0:T(1024)S(1)}, f32[1792]{0:T(1024)}, u32[]{:S(2)}) copy-start(f32[1792]{0:T(1024)} %get-tuple-element.545) | copy-start | bytes 21508
  75.2 7.3 %copy-start.77 = (f32[1792]{0:T(1024)S(1)}, f32[1792]{0:T(1024)}, u32[]{:S(2)}) copy-start(f32[1792]{0:T(1024)} %get-tuple-element.546) | copy-start | bytes 21508
  75.2 7.3 %copy-start.91 = (f32[1792]{0:T(1024)S(1)}, f32[1792]{0:T(1024)}, u32[]{:S(2)}) copy-start(f32[1792]{0:T(1024)} %reduce.9) | copy-start | bytes 21508
  75.2 6.0 %collective-permute-start.3 = (f32[3,1792]{1,0:T(4,128)S(1)}, f32[3,1792]{1,0:T(4,128)S(1)}, u32[]{:S(2)}, u32[]{:S(2)}) collective-permute-start(f32[3,1792]{1,0:T(4,128)S(1)} %copy.363), channel_id=1, source_target_pairs={{0,4},{4,8},{8,12},{12,16},{16,20},{20,24},{24,28},{1,5},{5,9},{9,... | collective-permute-start | bytes 64520 | tf_op jit(solution)/shard_map/ppermute | solution.py:21
  87.8 94.1 %copy-start.23 = (f32[128,1792]{0,1:T(8,128)}, f32[128,1792]{0,1:T(8,128)S(1)}, u32[]{:S(2)}) copy-start(f32[128,1792]{0,1:T(8,128)S(1)} %get-tuple-element.619) | copy-start | bytes 2752516
  103.5 38.7 %copy-start = (f32[2,24,64,128]{3,2,1,0:T(8,128)}, f32[2,24,64,128]{3,2,1,0:T(8,128)S(1)}, u32[]{:S(2)}) copy-start(f32[2,24,64,128]{3,2,1,0:T(8,128)S(1)} %get-tuple-element.878) | copy-start | bytes 4718596
  104.4 86.5 %all-gather.10.cloned.1.call-start = ((), (), s32[]{:S(2)}) async-start(), calls=%async_computation.5 | async-start | bytes 2949120 | tf_op jit(solution)/shard_map/all_gather | solution.py:182
  105.2 154.0 %all-gather.12.cloned.1.call-start = ((), (), s32[]{:S(2)}) async-start(), calls=%async_computation.6 | async-start | bytes 3538944 | tf_op jit(solution)/shard_map/all_gather | solution.py:50
  110.4 31.8 %copy-start.58 = (f32[128,24]{0,1:T(8,128)}, f32[128,24]{0,1:T(8,128)S(1)}, u32[]{:S(2)}) copy-start(f32[128,24]{0,1:T(8,128)S(1)} %copy.379) | copy-start | bytes 36868
  185.3 8.9 %copy-start.11 = (f32[128,1536]{0,1:T(8,128)}, f32[128,1536]{0,1:T(8,128)S(1)}, u32[]{:S(2)}) copy-start(f32[128,1536]{0,1:T(8,128)S(1)} %get-tuple-element.618) | copy-start | bytes 2359300
  198.9 152.7 %reduce-scatter.5.cloned.1.call-start = ((), (), s32[]{:S(2)}) async-start(), calls=%async_computation.3 | async-start | bytes 2949120 | tf_op jit(solution)/shard_map/reduce_scatter | solution.py:289
  223.5 179.5 %reduce-scatter.3.cloned.1.call-start = ((), (), s32[]{:S(2)}) async-start(), calls=%async_computation.2 | async-start | bytes 6635520 | tf_op jit(solution)/shard_map/reduce_scatter | solution.py:286
  278.1 7.2 %copy-start.51 = (f32[2,64,24]{1,2,0:T(8,128)S(1)}, f32[2,64,24]{1,2,0:T(8,128)}, u32[]{:S(2)}) copy-start(f32[2,64,24]{1,2,0:T(8,128)} %get-tuple-element.631) | copy-start | bytes 36868
  329.2 6.1 %collective-permute-start.4 = (f32[3,1792]{1,0:T(4,128)}, f32[3,1792]{1,0:T(4,128)}, u32[]{:S(2)}, u32[]{:S(2)}) collective-permute-start(f32[3,1792]{1,0:T(4,128)} %copy.407), channel_id=1, source_target_pairs={{4,0},{8,4},{12,8},{16,12},{20,16},{24,20},{28,24},{5,1},{9,5},{13... | collective-permute-start | bytes 64520 | tf_op jit(solution)/shard_map/ppermute | solution.py:21
  338.8 8.7 %copy-start.96 = (f32[128]{0:T(128)S(1)}, f32[128]{0:T(128)}, u32[]{:S(2)}) copy-start(f32[128]{0:T(128)} %copy-done.95) | copy-start | bytes 1540
  351.5 203.6 %all-reduce.19.cloned.1.call-start = ((), (), s32[]{:S(2)}) async-start(), calls=%async_computation.7 | async-start | bytes 7667712 | tf_op jit(solution)/shard_map/psum | solution.py:293
  410.6 49.0 %copy-start.112 = (f32[128]{0:T(128)S(1)}, f32[128]{0:T(128)}, u32[]{:S(2)}) copy-start(f32[128]{0:T(128)} %copy-done.111) | copy-start | bytes 1540
  410.7 49.0 %copy-start.38 = (bf16[1,128,768]{2,1,0:T(8,128)(2,1)S(1)}, bf16[1,128,768]{2,1,0:T(8,128)(2,1)}, u32[]{:S(2)}) copy-start(bf16[1,128,768]{2,1,0:T(8,128)(2,1)} %param.24) | copy-start | bytes 589828
  (99 other events, 297.7 us)
Sparse Core Ops, SparseCore 0:
  104.6 61.9 all-gather.7
  168.2 22.6 all-gather.9
  199.0 60.1 all-gather.11
  262.2 31.4 reduce-scatter.4
  351.6 51.3 reduce-scatter.2
  407.2 147.8 all-reduce.18
